TPU v7x, 32 devices: a whole 2x2x4 slice. The times are simulated.
32 devices in a mesh: rep: 2 (over y), shard: 16 (over z, x, core).
Axes of the slice: x: 2, y: 2, z: 4, core: 2. Of those that a mesh axis runs over, the one named last changes fastest.
Arguments:
- latents: bfloat16 [32, 128, 1152], P(('rep', 'shard')), may hold values from -5 to 5
- cond: float32 [32, 1152], P(('rep', 'shard')), may hold values from -6 to 6
- timesteps: int32 [32], P(('rep', 'shard')), may hold values from 0 to 999
- cotangent: bfloat16 [32, 128, 1152], P(('rep', 'shard')), may hold values from -6 to 6
- w_qkv: float32 [1152, 3456], P('shard'), may hold values from -0.11785113 to 0.11785113
- w_proj: float32 [1152, 1152], P('shard'), may hold values from -0.75 to 0.75
- w_fc1: float32 [1152, 4608], P('shard'), may hold values from -0.1875 to 0.1875
- w_fc2: float32 [4608, 1152], P('shard'), may hold values from -0.1875 to 0.1875
- w_ada: float32 [1152, 6912], P(None, 'shard'), may hold values from -0.015625 to 0.015625
- biases: float32 [16128], replicated, may hold values from -3 to 3
- m_qkv: float32 [1152, 3456], P('shard', 'rep'), may hold values from -0.00012272017 to 0.00012272017
- m_proj: float32 [1152, 1152], P('shard', 'rep'), may hold values from -0.00012272017 to 0.00012272017
- m_fc1: float32 [1152, 4608], P('shard', 'rep'), may hold values from -0.00012272017 to 0.00012272017
- m_fc2: float32 [4608, 1152], P('shard', 'rep'), may hold values from -0.00012272017 to 0.00012272017
- m_ada: float32 [1152, 6912], P('rep', 'shard'), may hold values from -0.00012272017 to 0.00012272017
- m_bias: float32 [16128], replicated, may hold values from -0.00012272017 to 0.00012272017
- v_qkv: float32 [1152, 3456], P('shard', 'rep'), may hold values from 4.1834e-11 to 1.67336e-10
- v_proj: float32 [1152, 1152], P('shard', 'rep'), may hold values from 4.1834e-11 to 1.67336e-10
- v_fc1: float32 [1152, 4608], P('shard', 'rep'), may hold values from 4.1834e-11 to 1.67336e-10
- v_fc2: float32 [4608, 1152], P('shard', 'rep'), may hold values from 4.1834e-11 to 1.67336e-10
- v_ada: float32 [1152, 6912], P('rep', 'shard'), may hold values from 4.1834e-11 to 1.67336e-10
- v_bias: float32 [16128], replicated, may hold values from 4.1834e-11 to 1.67336e-10
Outputs:
- block_out: float32 [32, 128, 1152], P(('rep', 'shard'))
- latents_grad: float32 [32, 128, 1152], P(('rep', 'shard'))
- cond_grad: float32 [32, 1152], P(('rep', 'shard'))
- new_qkv: float32 [1152, 3456], P('shard')
- new_proj: float32 [1152, 1152], P('shard')
- new_fc1: float32 [1152, 4608], P('shard')
- new_fc2: float32 [4608, 1152], P('shard')
- new_ada: float32 [1152, 6912], P(None, 'shard')
- bias_update: float32 [16128], replicated
- new_m_qkv: float32 [1152, 3456], P('shard', 'rep')
- new_m_proj: float32 [1152, 1152], P('shard', 'rep')
- new_m_fc1: float32 [1152, 4608], P('shard', 'rep')
- new_m_fc2: float32 [4608, 1152], P('shard', 'rep')
- new_m_ada: float32 [1152, 6912], P('rep', 'shard')
- new_m_bias: float32 [16128], replicated
- new_v_qkv: float32 [1152, 3456], P('shard', 'rep')
- new_v_proj: float32 [1152, 1152], P('shard', 'rep')
- new_v_fc1: float32 [1152, 4608], P('shard', 'rep')
- new_v_fc2: float32 [4608, 1152], P('shard', 'rep')
- new_v_ada: float32 [1152, 6912], P('rep', 'shard')
- new_v_bias: float32 [16128], replicated
All inputs are finite; a program needn't handle non-finite values.
Results may differ from a plain program's by a relative error of at most 0.014.
Values may be sent and summed in bfloat16 or wider, within the bound.
No kernel may reach another device: no remote copies, remote signals or barrier semaphores. Data moves between devices by JAX's collectives and lax.ppermute only.
A program may use at most 256 MiB of HBM per device.

v0:
```python
import math
import jax
import jax.numpy as jnp
from jax import lax
from jax.sharding import PartitionSpec as P

HD = 72
H = 16
FF = 4608
ln_eps = 1e-06
beta_one = 0.9
beta_two = 0.999
adam_eps = 1e-08
learn_rate = 0.03
decay_rate = 0.01
step_count = 2
gelu_coef = 0.044715


def product(form, left, right):
    return jnp.einsum(form, left, right, preferred_element_type=jnp.float32)


def normalize(rows):
    center = rows - jnp.mean(rows, axis=-1, keepdims=True)
    rstd = lax.rsqrt(jnp.mean(center * center, axis=-1, keepdims=True) + ln_eps)
    return (center * rstd, rstd)


def norm_back(grad, normed, rstd):
    return rstd * (
        grad
        - jnp.mean(grad, axis=-1, keepdims=True)
        - normed * jnp.mean(grad * normed, axis=-1, keepdims=True)
    )


def gelu_parts(pre):
    root = math.sqrt(2.0 / math.pi)
    inner = root * (pre + gelu_coef * pre * pre * pre)
    tangent = jnp.tanh(inner)
    value = 0.5 * pre * (1.0 + tangent)
    slope = 0.5 * (1.0 + tangent) + 0.5 * pre * (1.0 - tangent * tangent) * root * (
        1.0 + 3.0 * gelu_coef * pre * pre
    )
    return (value, slope)


def time_embed(steps, width):
    half = width // 2
    freqs = jnp.exp(-math.log(10000.0) * jnp.arange(half, dtype=jnp.float32) / half)
    angles = steps.astype(jnp.float32)[:, None] * freqs[None, :]
    return jnp.concatenate([jnp.cos(angles), jnp.sin(angles)], axis=1)


def block_pass(inputs, cotan, mod, wq_b, wp_b, w1_b, w2_b, biases):
    batch, length, width = inputs.shape
    inner = H * HD
    b_q = biases[0:inner]
    b_v = biases[inner : 2 * inner]
    b_proj = biases[2 * inner : 2 * inner + width]
    b_fc1 = biases[2 * inner + width : 2 * inner + width + FF]
    b_fc2 = biases[2 * inner + width + FF : 2 * inner + 2 * width + FF]
    parts = [mod[:, i * width : (i + 1) * width][:, None, :] for i in range(6)]
    shift1, scale1, gate1, shift2, scale2, gate2 = parts
    rows = inputs.astype(jnp.float32)
    n_one, r_one = normalize(rows)
    a_one = (n_one * (1.0 + scale1) + shift1).astype(jnp.bfloat16)
    qkv = product("bld,de->ble", a_one, wq_b)
    queries = (qkv[..., :inner] + b_q).astype(jnp.bfloat16).reshape(batch, length, H, HD)
    key_rows = qkv[..., inner : 2 * inner].astype(jnp.bfloat16).reshape(batch, length, H, HD)
    value_rows = (qkv[..., 2 * inner :] + b_v).astype(jnp.bfloat16).reshape(batch, length, H, HD)
    factor = HD ** (-0.5)
    scores = product("bqhd,bkhd->bhqk", queries, key_rows) * factor
    top = jnp.max(scores, axis=-1, keepdims=True)
    expo = jnp.exp(scores - top)
    probs = expo / jnp.sum(expo, axis=-1, keepdims=True)
    probs_b = probs.astype(jnp.bfloat16)
    heads_out = product("bhqk,bkhd->bqhd", probs_b, value_rows).astype(jnp.bfloat16)
    heads_flat = heads_out.reshape(batch, length, inner)
    attn = product("ble,ed->bld", heads_flat, wp_b) + b_proj
    x_one = rows + gate1 * attn
    n_two, r_two = normalize(x_one)
    a_two = (n_two * (1.0 + scale2) + shift2).astype(jnp.bfloat16)
    pre = product("bld,df->blf", a_two, w1_b) + b_fc1
    act_val, act_slope = gelu_parts(pre)
    act = act_val.astype(jnp.bfloat16)
    mlp = product("blf,fd->bld", act, w2_b) + b_fc2
    out = x_one + gate2 * mlp
    grad_out = cotan.astype(jnp.float32)
    d_gate2 = jnp.sum(grad_out * mlp, axis=1)
    d_mlp = grad_out * gate2
    d_mlp_b = d_mlp.astype(jnp.bfloat16)
    g_fc2 = product("blf,bld->fd", act, d_mlp_b)
    g_b_fc2 = jnp.sum(d_mlp, axis=(0, 1))
    d_pre = product("bld,fd->blf", d_mlp_b, w2_b) * act_slope
    d_pre_b = d_pre.astype(jnp.bfloat16)
    g_fc1 = product("bld,blf->df", a_two, d_pre_b)
    g_b_fc1 = jnp.sum(d_pre, axis=(0, 1))
    d_a2 = product("blf,df->bld", d_pre_b, w1_b)
    d_shift2 = jnp.sum(d_a2, axis=1)
    d_scale2 = jnp.sum(d_a2 * n_two, axis=1)
    dx_one = grad_out + norm_back(d_a2 * (1.0 + scale2), n_two, r_two)
    d_gate1 = jnp.sum(dx_one * attn, axis=1)
    d_attn = dx_one * gate1
    d_attn_b = d_attn.astype(jnp.bfloat16)
    g_proj = product("ble,bld->ed", heads_flat, d_attn_b)
    g_b_proj = jnp.sum(d_attn, axis=(0, 1))
    d_heads = (
        product("bld,ed->ble", d_attn_b, wp_b).astype(jnp.bfloat16).reshape(batch, length, H, HD)
    )
    delta = jnp.sum(d_heads.astype(jnp.float32) * heads_out.astype(jnp.float32), axis=-1)
    delta = jnp.transpose(delta, (0, 2, 1))[..., None]
    d_probs = product("bqhd,bkhd->bhqk", d_heads, value_rows)
    d_scores = (probs * (d_probs - delta) * factor).astype(jnp.bfloat16)
    d_q = product("bhqk,bkhd->bqhd", d_scores, key_rows)
    d_k = product("bhqk,bqhd->bkhd", d_scores, queries)
    d_v = product("bhqk,bqhd->bkhd", probs_b, d_heads)
    g_b_q = jnp.sum(d_q, axis=(0, 1)).reshape(inner)
    g_b_v = jnp.sum(d_v, axis=(0, 1)).reshape(inner)
    d_qkv = jnp.concatenate(
        [
            d_q.reshape(batch, length, inner),
            d_k.reshape(batch, length, inner),
            d_v.reshape(batch, length, inner),
        ],
        axis=-1,
    ).astype(jnp.bfloat16)
    g_qkv = product("bld,ble->de", a_one, d_qkv)
    d_a1 = product("ble,de->bld", d_qkv, wq_b)
    d_shift1 = jnp.sum(d_a1, axis=1)
    d_scale1 = jnp.sum(d_a1 * n_one, axis=1)
    d_input = dx_one + norm_back(d_a1 * (1.0 + scale1), n_one, r_one)
    d_mod = jnp.concatenate([d_shift1, d_scale1, d_gate1, d_shift2, d_scale2, d_gate2], axis=1)
    bias_grad = jnp.concatenate([g_b_q, g_b_v, g_b_proj, g_b_fc1, g_b_fc2])
    return (out, d_input, d_mod, (g_qkv, g_proj, g_fc1, g_fc2), bias_grad)


def adam_change(weight, grad, first, second, clip):
    scaled = grad * clip
    first_new = beta_one * first + (1.0 - beta_one) * scaled
    second_new = beta_two * second + (1.0 - beta_two) * scaled * scaled
    first_hat = first_new / (1.0 - beta_one**step_count)
    second_hat = second_new / (1.0 - beta_two**step_count)
    change = -learn_rate * (first_hat / (jnp.sqrt(second_hat) + adam_eps) + decay_rate * weight)
    return (change, first_new, second_new)


def adam_step(weight, grad, first, second, clip):
    change, first_new, second_new = adam_change(weight, grad, first, second, clip)
    return (weight + change, first_new, second_new)


def shards(
    latents,
    cond,
    timesteps,
    cotangent,
    w_qkv,
    w_proj,
    w_fc1,
    w_fc2,
    w_ada,
    biases,
    m_qkv,
    m_proj,
    m_fc1,
    m_fc2,
    m_ada,
    m_bias,
    v_qkv,
    v_proj,
    v_fc1,
    v_fc2,
    v_ada,
    v_bias,
):
    width = cond.shape[1]
    b_ada = biases[biases.shape[0] - 6 * width :]
    cvec = cond + time_embed(timesteps, width)
    silu_c = jax.nn.silu(cvec).astype(jnp.bfloat16)
    ada_local = w_ada.astype(jnp.bfloat16)
    silu_group = lax.all_gather(silu_c, "shard", axis=0, tiled=True)
    mod_cols = jnp.dot(silu_group, ada_local, preferred_element_type=jnp.float32)
    mod = lax.all_to_all(mod_cols, "shard", split_axis=0, concat_axis=1, tiled=True) + b_ada
    wq_b, wp_b = (
        lax.all_gather(w_qkv.astype(jnp.bfloat16), "shard", axis=0, tiled=True),
        lax.all_gather(w_proj.astype(jnp.bfloat16), "shard", axis=0, tiled=True),
    )
    w1_b, w2_b = (
        lax.all_gather(w_fc1.astype(jnp.bfloat16), "shard", axis=0, tiled=True),
        lax.all_gather(w_fc2.astype(jnp.bfloat16), "shard", axis=0, tiled=True),
    )
    block_out, latents_grad, d_mod, grads, bias_head = block_pass(
        latents, cotangent, mod, wq_b, wp_b, w1_b, w2_b, biases
    )
    d_mod_b = d_mod.astype(jnp.bfloat16)
    d_mod_cols = lax.all_to_all(d_mod_b, "shard", split_axis=1, concat_axis=0, tiled=True)
    g_ada = jnp.dot(silu_group.T, d_mod_cols, preferred_element_type=jnp.float32)
    silu_terms = jnp.dot(d_mod_cols, ada_local.T, preferred_element_type=jnp.float32)
    silu_grad = lax.psum_scatter(silu_terms, "shard", scatter_dimension=0, tiled=True)
    sig = jax.nn.sigmoid(cvec)
    cond_grad = silu_grad * sig * (1.0 + cvec * (1.0 - sig))
    g_qkv, g_proj = (
        lax.psum_scatter(
            grads[0].astype(jnp.bfloat16), "shard", scatter_dimension=0, tiled=True
        ).astype(jnp.float32),
        lax.psum_scatter(
            grads[1].astype(jnp.bfloat16), "shard", scatter_dimension=0, tiled=True
        ).astype(jnp.float32),
    )
    g_fc1, g_fc2 = (
        lax.psum_scatter(
            grads[2].astype(jnp.bfloat16), "shard", scatter_dimension=0, tiled=True
        ).astype(jnp.float32),
        lax.psum_scatter(
            grads[3].astype(jnp.bfloat16), "shard", scatter_dimension=0, tiled=True
        ).astype(jnp.float32),
    )
    pieces = (
        lax.psum_scatter(g_qkv, "rep", scatter_dimension=1, tiled=True),
        lax.psum_scatter(g_proj, "rep", scatter_dimension=1, tiled=True),
        lax.psum_scatter(g_fc1, "rep", scatter_dimension=1, tiled=True),
        lax.psum_scatter(g_fc2, "rep", scatter_dimension=1, tiled=True),
        lax.psum_scatter(g_ada, "rep", scatter_dimension=0, tiled=True),
    )
    bias_partial = jnp.concatenate([bias_head, jnp.sum(d_mod, axis=0)])
    weight_squares = sum((jnp.sum(p * p) for p in pieces))
    g_bias, total_squares = lax.psum((bias_partial, weight_squares), ("rep", "shard"))
    gnorm = jnp.sqrt(total_squares + jnp.sum(g_bias * g_bias))
    clip = 1.0 / jnp.maximum(gnorm, 1.0)
    rank = lax.axis_index("rep")
    replicas = lax.axis_size("rep")
    weights = (w_qkv, w_proj, w_fc1, w_fc2, w_ada)
    dims = (1, 1, 1, 1, 0)
    firsts = (m_qkv, m_proj, m_fc1, m_fc2, m_ada)
    seconds = (v_qkv, v_proj, v_fc1, v_fc2, v_ada)
    new_pieces = []
    new_m = []
    new_v = []
    for weight, dim, grad, first, second in zip(weights, dims, pieces, firsts, seconds):
        count = weight.shape[dim] // replicas
        own = lax.dynamic_slice_in_dim(weight, rank * count, count, dim)
        updated, first_new, second_new = adam_step(own, grad, first, second, clip)
        new_pieces.append(updated)
        new_m.append(first_new)
        new_v.append(second_new)
    new_qkv, new_proj, new_fc1, new_fc2, new_ada = (
        lax.all_gather(new_pieces[0], "rep", axis=1, tiled=True),
        lax.all_gather(new_pieces[1], "rep", axis=1, tiled=True),
        lax.all_gather(new_pieces[2], "rep", axis=1, tiled=True),
        lax.all_gather(new_pieces[3], "rep", axis=1, tiled=True),
        lax.all_gather(new_pieces[4], "rep", axis=0, tiled=True),
    )
    bias_update, new_m_bias, new_v_bias = adam_change(biases, g_bias, m_bias, v_bias, clip)
    return (
        block_out,
        latents_grad,
        cond_grad,
        new_qkv,
        new_proj,
        new_fc1,
        new_fc2,
        new_ada,
        bias_update,
        new_m[0],
        new_m[1],
        new_m[2],
        new_m[3],
        new_m[4],
        new_m_bias,
        new_v[0],
        new_v[1],
        new_v[2],
        new_v[3],
        new_v[4],
        new_v_bias,
    )


def solution(mesh):
    in_specs = (
        P(("rep", "shard"), None, None),
        P(("rep", "shard"), None),
        P(("rep", "shard")),
        P(("rep", "shard"), None, None),
        P("shard", None),
        P("shard", None),
        P("shard", None),
        P("shard", None),
        P(None, "shard"),
        P(),
        P("shard", "rep"),
        P("shard", "rep"),
        P("shard", "rep"),
        P("shard", "rep"),
        P("rep", "shard"),
        P(),
        P("shard", "rep"),
        P("shard", "rep"),
        P("shard", "rep"),
        P("shard", "rep"),
        P("rep", "shard"),
        P(),
    )
    out_specs = (
        P(("rep", "shard"), None, None),
        P(("rep", "shard"), None, None),
        P(("rep", "shard"), None),
        P("shard", None),
        P("shard", None),
        P("shard", None),
        P("shard", None),
        P(None, "shard"),
        P(),
        P("shard", "rep"),
        P("shard", "rep"),
        P("shard", "rep"),
        P("shard", "rep"),
        P("rep", "shard"),
        P(),
        P("shard", "rep"),
        P("shard", "rep"),
        P("shard", "rep"),
        P("shard", "rep"),
        P("rep", "shard"),
        P(),
    )
    return jax.shard_map(shards, mesh=mesh, in_specs=in_specs, out_specs=out_specs, check_vma=False)
```

profile of v0, /device:TPU:0, one launch (start us, length us, event | category | flops | bytes accessed | tf_op | source)
XLA Modules:
  0.0 1095.6 jit_solution(5412278712987913531)
XLA Ops:
  11.1 2.4 convert_element_type.150
  17.3 24.2 %all-gather = bf16[16,1,1152]{2,1,0:T(2,128)(2,1)S(1)} all-gather(bf16[1,1,1152]{2,1,0:T(2,128)(2,1)S(1)} %get-tuple-element.62), channel_id=1, replica_groups=mesh['rep'=2,'shard'=16] {'shard'}, dimensions={0}, use_global_device_ids=true | all-gather | bytes 39168 | tf_op jit(solution)/shard_map/all_gather | solution.py:183
  42.8 3.5 all-to-all-start
  48.0 5.4 all-to-all-done
  54.2 31.5 %all-gather.13.cloned.1.call-done = bf16[1152,3456]{1,0:T(8,128)(2,1)} async-done(((bf16[72,3456]{1,0:T(8,128)(2,1)}), bf16[1152,3456]{1,0:T(8,128)(2,1)}) %all-gather.13.cloned.1.call-update) | async-done | bytes 7962640 | tf_op jit(solution)/shard_map/all_gather | solution.py:187
  85.7 4.7 convolution_bitcast_fusion
  92.1 38.2 %all-gather.15.cloned.1.call-done = bf16[1152,1152]{1,0:T(8,128)(2,1)} async-done(((bf16[72,1152]{1,0:T(8,128)(2,1)}), bf16[1152,1152]{1,0:T(8,128)(2,1)}) %all-gather.15.cloned.1.call-update) | async-done | bytes 2654224 | tf_op jit(solution)/shard_map/all_gather | solution.py:188
  130.3 3.2 fusion.88
  134.3 86.1 %all-gather.17.cloned.1.call-done = bf16[1152,4608]{1,0:T(8,128)(2,1)} async-done(((bf16[72,4608]{1,0:T(8,128)(2,1)}), bf16[1152,4608]{1,0:T(8,128)(2,1)}) %all-gather.17.cloned.1.call-update) | async-done | bytes 10616848 | tf_op jit(solution)/shard_map/all_gather | solution.py:191
  220.4 5.8 convolution_add_fusion
  226.2 83.5 %all-gather.19.cloned.1.call-done = bf16[4608,1152]{1,0:T(8,128)(2,1)} async-done(((bf16[288,1152]{1,0:T(8,128)(2,1)}), bf16[4608,1152]{1,0:T(8,128)(2,1)}) %all-gather.19.cloned.1.call-update) | async-done | bytes 10616848 | tf_op jit(solution)/shard_map/all_gather | solution.py:192
  309.7 8.6 fusion.93
  318.4 4.0 fusion.33
  323.2 8.2 fusion.19
  332.2 2.3 convolution_convert_fusion.3
  334.6 3.6 convolution_convert_fusion.4
  348.8 5.6 convolution_convert_fusion.2
  354.4 6.7 convolution_convert_fusion
  362.4 5.8 convolution_convert_fusion.1
  369.2 6.5 fusion.28
  378.8 9.4 all_to_all.29
  390.3 5.6 reduce-scatter.38.cloned.1.call-done
  397.9 99.9 %reduce-scatter.36.cloned.1.call-done = bf16[72,3456]{1,0:T(8,128)(2,1)} async-done(((bf16[1152,3456]{1,0:T(8,128)(2,1)}), bf16[72,3456]{1,0:T(8,128)(2,1)}) %reduce-scatter.36.cloned.1.call-update) | async-done | bytes 497680
  497.8 2.5 copy.107
  500.4 121.8 %reduce-scatter.26.cloned.1.call-done = bf16[288,1152]{1,0:T(8,128)(2,1)} async-done(((bf16[4608,1152]{1,0:T(8,128)(2,1)}), bf16[288,1152]{1,0:T(8,128)(2,1)}) %reduce-scatter.26.cloned.1.call-update) | async-done | bytes 663568 | tf_op jit(solution)/shard_map/reduce_scatter | solution.py:216
  622.2 2.6 copy.111
  624.9 121.7 %reduce-scatter.22.cloned.1.call-done = bf16[72,4608]{1,0:T(8,128)(2,1)} async-done(((bf16[1152,4608]{1,0:T(8,128)(2,1)}), bf16[72,4608]{1,0:T(8,128)(2,1)}) %reduce-scatter.22.cloned.1.call-update) | async-done | bytes 663568 | tf_op jit(solution)/shard_map/reduce_scatter | solution.py:213
  750.2 33.1 %reduce-scatter.34.cloned.1.call-done = f32[576,432]{1,0:T(8,128)} async-done(((f32[1152,432]{1,0:T(8,128)}), f32[576,432]{1,0:T(8,128)}) %reduce-scatter.34.cloned.1.call-update) | async-done | bytes 995344
  785.8 15.5 %reduce-scatter.30.cloned.1.call-done = f32[576,72]{1,0:T(8,128)} async-done(((f32[1152,72]{1,0:T(8,128)}), f32[576,72]{1,0:T(8,128)}) %reduce-scatter.30.cloned.1.call-update) | async-done | bytes 165904
  804.7 27.8 %reduce-scatter.28.cloned.1.call-done = f32[1728,72]{1,0:T(8,128)} async-done(((f32[3456,72]{1,0:T(8,128)}), f32[1728,72]{1,0:T(8,128)}) %reduce-scatter.28.cloned.1.call-update) | async-done | bytes 497680
  837.8 25.2 %reduce-scatter.32.cloned.1.call-done = f32[576,288]{1,0:T(8,128)} async-done(((f32[1152,288]{1,0:T(8,128)}), f32[576,288]{1,0:T(8,128)}) %reduce-scatter.32.cloned.1.call-update) | async-done | bytes 663568
  863.0 2.3 copy.112
  867.2 22.1 %reduce-scatter.24.cloned.1.call-done = f32[72,2304]{1,0:T(8,128)} async-done(((f32[72,4608]{1,0:T(8,128)}), f32[72,2304]{1,0:T(8,128)}) %reduce-scatter.24.cloned.1.call-update) | async-done | bytes 663568 | tf_op jit(solution)/shard_map/reduce_scatter | solution.py:223
  893.2 40.0 %all-reduce.3 = (f32[]{:T(128)}, f32[16128]{0:T(1024)S(1)}) all-reduce(f32[]{:T(128)S(6)} %add.349, f32[16128]{0:T(1024)S(1)} %constant_dynamic-update-slice_fusion.10), channel_id=1, replica_groups=mesh['rep'=2,'shard'=16] {'rep','shard'}, use_global_device_ids=true, to_apply=%region_32.33 | all-reduce | flops 16129 | bytes 129032 | tf_op jit(solution)/shard_map/psum | solution.py:229
  935.2 3.8 add_bitcast_fusion.1
  939.7 3.3 multiply_add_fusion.3
  943.1 2.4 fusion.27
  945.6 3.9 add_bitcast_fusion
  949.5 30.8 %all-reduce.6.cloned.1.call-done = f32[16,1152]{1,0:T(8,128)} async-done(((f32[16,1152]{1,0:T(8,128)}), f32[16,1152]{1,0:T(8,128)}) %all-reduce.6.cloned.1.call-update) | async-done | bytes 73744
  982.3 2.9 add_bitcast_fusion.2
  985.2 21.1 %all-gather.1 = f32[2,1728,72]{1,2,0:T(8,128)S(1)} all-gather(f32[1,1728,72]{1,2,0:T(8,128)S(1)} %get-tuple-element.56), channel_id=1, replica_groups=mesh['rep'=2,'shard'=16] {'rep'}, dimensions={0}, use_global_device_ids=true | all-gather | bytes 1492992 | tf_op jit(solution)/shard_map/all_gather | solution.py:249
  1009.5 9.2 all-gather.2
  1020.6 2.5 copy.100
  1025.1 19.7 %all-gather.21.cloned.1.call-done = f32[72,4608]{1,0:T(8,128)} async-done(((f32[72,2304]{1,0:T(8,128)}), f32[72,4608]{1,0:T(8,128)}) %all-gather.21.cloned.1.call-update) | async-done | bytes 1327120 | tf_op jit(solution)/shard_map/all_gather | solution.py:251
  1044.9 36.4 %all-gather.25.cloned.1.call-done = f32[2,576,432]{1,2,0:T(8,128)} async-done(((f32[1,576,432]{1,2,0:T(8,128)}), f32[2,576,432]{1,2,0:T(8,128)}) %all-gather.25.cloned.1.call-update) | async-done | bytes 1990672 | tf_op jit(solution)/shard_map/all_gather | solution.py:253
  1081.2 2.8 copy.101
  1084.0 2.4 reshape.469
  1086.4 2.5 copy.147
  (256 shorter events, 62.6 us)
Async XLA Ops:
  7.2 78.5 %all-gather.13.cloned.1.call-start = ((), (), s32[]{:S(2)}) async-start(), calls=%async_computation.11 | async-start | bytes 8460288 | tf_op jit(solution)/shard_map/all_gather | solution.py:187
  9.3 121.0 %all-gather.15.cloned.1.call-start = ((), (), s32[]{:S(2)}) async-start(), calls=%async_computation.12 | async-start | bytes 2820096 | tf_op jit(solution)/shard_map/all_gather | solution.py:188
  11.0 5.6 copy-start.60
  11.1 30.5 %copy-start.2 = (f32[1152,432]{0,1:T(8,128)S(1)}, f32[1152,432]{0,1:T(8,128)}, u32[]{:S(2)}) copy-start(f32[1152,432]{0,1:T(8,128)} %param.30) | copy-start | bytes 5971972
  11.1 209.3 %all-gather.17.cloned.1.call-start = ((), (), s32[]{:S(2)}) async-start(), calls=%async_computation.13 | async-start | bytes 11280384 | tf_op jit(solution)/shard_map/all_gather | solution.py:191
  13.5 32.8 %copy-start.1 = (bf16[1,128,1152]{2,1,0:T(8,128)(2,1)S(1)}, bf16[1,128,1152]{2,1,0:T(8,128)(2,1)}, u32[]{:S(2)}) copy-start(bf16[1,128,1152]{2,1,0:T(8,128)(2,1)} %param.22) | copy-start | bytes 884740
  13.5 33.2 %copy-start.18 = (f32[16128]{0:T(1024)S(1)}, f32[16128]{0:T(1024)}, u32[]{:S(2)}) copy-start(f32[16128]{0:T(1024)} %param.31) | copy-start | bytes 193540
  13.5 296.2 %all-gather.19.cloned.1.call-start = ((), (), s32[]{:S(2)}) async-start(), calls=%async_computation.14 | async-start | bytes 11280384 | tf_op jit(solution)/shard_map/all_gather | solution.py:192
  42.8 10.6 all-to-all-start
  46.3 349.6 %reduce-scatter.38.cloned.1.call-start = ((), (), s32[]{:S(2)}) async-start(), calls=%async_computation.27 | async-start | bytes 2820096
  46.5 43.9 %copy-start.41 = (f32[128]{0:T(128)}, f32[128]{0:T(128)S(1)}, u32[]{:S(2)}) copy-start(f32[128]{0:T(128)S(1)} %broadcast_multiply_fusion.5) | copy-start | bytes 1540
  47.3 43.1 %copy-start.49 = (f32[128]{0:T(128)}, f32[128]{0:T(128)S(1)}, u32[]{:S(2)}) copy-start(f32[128]{0:T(128)S(1)} %add_rsqrt_fusion.1) | copy-start | bytes 1540
  54.2 36.2 %copy-start.27 = (f32[1152]{0:T(1024)}, f32[1152]{0:T(1024)S(1)}, u32[]{:S(2)}) copy-start(f32[1152]{0:T(1024)S(1)} %get-tuple-element.36) | copy-start | bytes 13828
  54.2 76.1 %copy-start.32 = (f32[1152]{0:T(1024)}, f32[1152]{0:T(1024)S(1)}, u32[]{:S(2)}) copy-start(f32[1152]{0:T(1024)S(1)} %get-tuple-element.38) | copy-start | bytes 13828
  91.8 38.6 %copy-start.66 = (f32[16,128]{1,0:T(8,128)}, f32[16,128]{1,0:T(8,128)S(1)}, u32[]{:S(2)}) copy-start(f32[16,128]{1,0:T(8,128)S(1)} %get-tuple-element.79) | copy-start | bytes 24580
  91.8 41.8 %copy-start.64 = (f32[16,128,128]{1,2,0:T(8,128)}, f32[16,128,128]{1,2,0:T(8,128)S(1)}, u32[]{:S(2)}) copy-start(f32[16,128,128]{1,2,0:T(8,128)S(1)} %get-tuple-element.80) | copy-start | bytes 3145732
  133.6 86.9 %copy-start.46 = (f32[128]{0:T(128)}, f32[128]{0:T(128)S(1)}, u32[]{:S(2)}) copy-start(f32[128]{0:T(128)S(1)} %broadcast_multiply_fusion.4) | copy-start | bytes 1540
  309.7 8.6 copy-start
  309.7 8.6 copy-start.47
  309.7 8.6 copy-start.52
  334.5 163.3 %reduce-scatter.36.cloned.1.call-start = ((), (), s32[]{:S(2)}) async-start(), calls=%async_computation.26 | async-start | bytes 8460288
  354.4 267.8 %reduce-scatter.26.cloned.1.call-start = ((), (), s32[]{:S(2)}) async-start(), calls=%async_computation.17 | async-start | bytes 11280384 | tf_op jit(solution)/shard_map/reduce_scatter | solution.py:216
  361.1 385.5 %reduce-scatter.22.cloned.1.call-start = ((), (), s32[]{:S(2)}) async-start(), calls=%async_computation.15 | async-start | bytes 11280384 | tf_op jit(solution)/shard_map/reduce_scatter | solution.py:213
  368.2 9.0 copy-start.58
  368.2 9.0 copy-start.38
  368.2 9.0 copy-start.39
  368.2 9.1 copy-start.57
  368.2 20.1 %copy-start.25 = (bf16[16,1,1152]{2,1,0:T(2,128)(2,1)S(1)}, bf16[16,1,1152]{2,1,0:T(2,128)(2,1)}, u32[]{:S(2)}) copy-start(bf16[16,1,1152]{2,1,0:T(2,128)(2,1)} %copy-done.24) | copy-start | bytes 110596
  368.2 415.1 %reduce-scatter.34.cloned.1.call-start = ((), (), s32[]{:S(2)}) async-start(), calls=%async_computation.24 | async-start | bytes 3538944
  390.3 411.1 %reduce-scatter.30.cloned.1.call-start = ((), (), s32[]{:S(2)}) async-start(), calls=%async_computation.22 | async-start | bytes 884736
  397.8 434.7 %reduce-scatter.28.cloned.1.call-start = ((), (), s32[]{:S(2)}) async-start(), calls=%async_computation.21 | async-start | bytes 2654208
  500.4 362.6 %reduce-scatter.32.cloned.1.call-start = ((), (), s32[]{:S(2)}) async-start(), calls=%async_computation.23 | async-start | bytes 2654208
  624.8 124.2 %copy-start.37 = (f32[16,72]{1,0:T(8,128)S(1)}, f32[16,72]{1,0:T(8,128)}, u32[]{:S(2)}) copy-start(f32[16,72]{1,0:T(8,128)} %get-tuple-element.73) | copy-start | bytes 13828
  624.8 124.3 %copy-start.56 = (f32[16,72]{1,0:T(8,128)S(1)}, f32[16,72]{1,0:T(8,128)}, u32[]{:S(2)}) copy-start(f32[16,72]{1,0:T(8,128)} %get-tuple-element.71) | copy-start | bytes 13828
  624.8 124.4 %copy-start.55 = (f32[1152]{0:T(1024)S(1)}, f32[1152]{0:T(1024)}, u32[]{:S(2)}) copy-start(f32[1152]{0:T(1024)} %get-tuple-element.69) | copy-start | bytes 13828
  624.8 124.5 %copy-start.40 = (f32[4608]{0:T(1024)S(1)}, f32[4608]{0:T(1024)}, u32[]{:S(2)}) copy-start(f32[4608]{0:T(1024)} %get-tuple-element.86) | copy-start | bytes 55300
  624.8 124.5 %copy-start.54 = (f32[1152]{0:T(1024)S(1)}, f32[1152]{0:T(1024)}, u32[]{:S(2)}) copy-start(f32[1152]{0:T(1024)} %get-tuple-element.31) | copy-start | bytes 13828
  624.8 124.5 %copy-start.3 = (f32[1152,432]{0,1:T(8,128)S(1)}, f32[1152,432]{0,1:T(8,128)}, u32[]{:S(2)}) copy-start(f32[1152,432]{0,1:T(8,128)} %param.30) | copy-start | bytes 5971972
  624.9 264.5 %reduce-scatter.24.cloned.1.call-start = ((), (), s32[]{:S(2)}) async-start(), calls=%async_computation.16 | async-start | bytes 1990656 | tf_op jit(solution)/shard_map/reduce_scatter | solution.py:223
  748.9 231.4 %all-reduce.6.cloned.1.call-start = ((), (), s32[]{:S(2)}) async-start(), calls=%async_computation.25 | async-start | bytes 147456
  893.2 127.4 %all-gather.23.cloned.1.call-start = ((), (), s32[]{:S(2)}) async-start(), calls=%async_computation.19 | async-start | bytes 2211840 | tf_op jit(solution)/shard_map/all_gather | solution.py:252
  939.0 105.8 %all-gather.21.cloned.1.call-start = ((), (), s32[]{:S(2)}) async-start(), calls=%async_computation.18 | async-start | bytes 1990656 | tf_op jit(solution)/shard_map/all_gather | solution.py:251
  943.0 138.2 %all-gather.25.cloned.1.call-start = ((), (), s32[]{:S(2)}) async-start(), calls=%async_computation.20 | async-start | bytes 3317760 | tf_op jit(solution)/shard_map/all_gather | solution.py:253
  945.5 34.7 %copy-start.44 = (f32[1,1152]{1,0:T(1,128)S(1)}, f32[1,1152]{1,0:T(1,128)}, u32[]{:S(2)}) copy-start(f32[1,1152]{1,0:T(1,128)} %get-tuple-element.63) | copy-start | bytes 13828
  945.5 34.7 %copy-start.45 = (f32[1,1152]{1,0:T(1,128)S(1)}, f32[1,1152]{1,0:T(1,128)}, u32[]{:S(2)}) copy-start(f32[1,1152]{1,0:T(1,128)} %get-tuple-element.64) | copy-start | bytes 13828
  1006.8 13.1 %copy-start.19 = (f32[16128]{0:T(1024)S(1)}, f32[16128]{0:T(1024)}, u32[]{:S(2)}) copy-start(f32[16128]{0:T(1024)} %param.31) | copy-start | bytes 193540
  1006.8 13.1 %copy-start.34 = (f32[16128]{0:T(1024)S(1)}, f32[16128]{0:T(1024)}, u32[]{:S(2)}) copy-start(f32[16128]{0:T(1024)} %param.37) | copy-start | bytes 193540
  1006.8 13.1 %copy-start.35 = (f32[16128]{0:T(1024)S(1)}, f32[16128]{0:T(1024)}, u32[]{:S(2)}) copy-start(f32[16128]{0:T(1024)} %param.43) | copy-start | bytes 193540
  (38 other events, 92.1 us)
Sparse Core Ops, SparseCore 0:
  10.7 74.9 all-gather.12
  88.5 41.8 all-gather.14
  133.2 87.1 all-gather.16
  223.1 86.5 all-gather.18
  334.6 61.2 reduce-scatter.37
  399.8 97.9 reduce-scatter.35
  501.9 120.2 reduce-scatter.25
  626.3 120.2 reduce-scatter.21
  748.9 34.3 reduce-scatter.33
  786.0 15.3 reduce-scatter.29
  804.2 28.2 reduce-scatter.27
  834.6 28.3 reduce-scatter.31
  865.8 23.4 reduce-scatter.23
  893.3 86.9 all-reduce.5
  982.2 35.7 all-gather.22
  1019.9 24.8 all-gather.20
  1046.8 34.3 all-gather.24
where the time goes:
time: 1110 us; the launch traced here: 1100 us
  waiting for transfers between devices  804 us (72%)
  blocking collectives  104 us (9%)
  matrix products  73.8 us (7%)
  other arithmetic  45.3 us (4%)
  local copies, waits for them, and re-layouts  43.6 us (4%)
  between operations  20.3 us (2%)
    unnamed x24, waiting for transfers between devices  238 us
    reduce_scatter x1, waiting for transfers between devices, shards(): lax.psum_scatter(grads[3].astype(jnp.bfloat16), 'shard', scatter_dimensio...  122 us
    reduce_scatter x1, waiting for transfers between devices, shards(): lax.psum_scatter(grads[2].astype(jnp.bfloat16), 'shard', scatter_dimensio...  122 us
    all_gather x1, waiting for transfers between devices, shards(): lax.all_gather(w_fc1.astype(jnp.bfloat16), 'shard', axis=0, tiled=True)  86.1 us
    all_gather x1, waiting for transfers between devices, shards(): lax.all_gather(w_fc2.astype(jnp.bfloat16), 'shard', axis=0, tiled=True)  83.5 us
    dot_general x17, matrix products, product(): return jnp.einsum(form, left, right, preferred_element_type=jnp.float32)  70.1 us
    psum x1, blocking collectives, shards(): lax.psum((bias_partial, weight_squares), ('rep', 'shard'))  40 us
    all_gather x1, waiting for transfers between devices, shards(): lax.all_gather(w_proj.astype(jnp.bfloat16), 'shard', axis=0, tiled=True)  38.2 us
  transfers between devices with their start and end apart: 18, of which 17 were waited for; matrix products, arithmetic and copies ran while one was open for 11% of the time, Pallas kernels for 0%

commit v1 on v0

--- a/solution.py
+++ b/solution.py
@@ -15,6 +15,27 @@
 decay_rate = 0.01
 step_count = 2
 gelu_coef = 0.044715
+
+
+def collect(x, axis, dim):
+    size, index, extent = (lax.axis_size(axis), lax.axis_index(axis), x.shape[dim])
+    right = [(i, (i + 1) % size) for i in range(size)]
+    left = [(i, (i - 1) % size) for i in range(size)]
+    result = jnp.zeros((*x.shape[:dim], size * extent, *x.shape[dim + 1 :]), x.dtype)
+    result = lax.dynamic_update_slice_in_dim(result, x, index * extent, axis=dim)
+    from_left = from_right = x
+    half = size // 2
+    for step in range(1, half + 1):
+        from_left = lax.ppermute(from_left, axis, right)
+        result = lax.dynamic_update_slice_in_dim(
+            result, from_left, (index - step) % size * extent, axis=dim
+        )
+        if step < size - half:
+            from_right = lax.ppermute(from_right, axis, left)
+            result = lax.dynamic_update_slice_in_dim(
+                result, from_right, (index + step) % size * extent, axis=dim
+            )
+    return result
 
 
 def product(form, left, right):
@@ -180,7 +201,7 @@
     cvec = cond + time_embed(timesteps, width)
     silu_c = jax.nn.silu(cvec).astype(jnp.bfloat16)
     ada_local = w_ada.astype(jnp.bfloat16)
-    silu_group = lax.all_gather(silu_c, "shard", axis=0, tiled=True)
+    silu_group = collect(silu_c, "shard", 0)
     mod_cols = jnp.dot(silu_group, ada_local, preferred_element_type=jnp.float32)
     mod = lax.all_to_all(mod_cols, "shard", split_axis=0, concat_axis=1, tiled=True) + b_ada
     wq_b, wp_b = (

time: 1110 us -> 1100 us (level)
  starting transfers between devices: 4.38 us -> 37.8 us
  blocking collectives: 104 us -> 79.6 us
    ppermute x0 -> x15, starting transfers between devices: none -> 32.9 us  [the longest x7 32.4 us: collect(): from_right = lax.ppermute(from_right, axis, left)]
    all_gather x1 -> x0, blocking collectives: 24.2 us -> none  [shards(): silu_group = lax.all_gather(silu_c, 'shard', axis=0, tiled=True)]
    all_gather x1, waiting for transfers between devices: 31.5 us -> 9.55 us  [shards(): lax.all_gather(w_qkv.astype(jnp.bfloat16), 'shard', axis=0, tiled=True)]
    ppermute x0 -> x15, waiting for transfers between devices: none -> 13.2 us  [the longest x8 11.6 us: collect(): from_left = lax.ppermute(from_left, axis, right)]
  transfers between devices with their start and end apart: 18 -> 33, of which waited for: 17 -> 30; matrix products, arithmetic and copies ran while one was open for 11% -> 11% of each run, Pallas kernels for 0% -> 0%
where the time goes in v1:
time: 1100 us
  waiting for transfers between devices  793 us (72%)
  blocking collectives  79.6 us (7%)
  matrix products  75.8 us (7%)
  local copies, waits for them, and re-layouts  44.5 us (4%)
  other arithmetic  44 us (4%)
  starting transfers between devices  37.8 us (3%)
  between operations  20.6 us (2%)
    unnamed x24, waiting for transfers between devices  238 us
    reduce_scatter x1, waiting for transfers between devices, shards(): lax.psum_scatter(grads[3].astype(jnp.bfloat16), 'shard', scatter_dimensio...  122 us
    reduce_scatter x1, waiting for transfers between devices, shards(): lax.psum_scatter(grads[2].astype(jnp.bfloat16), 'shard', scatter_dimensio...  122 us
    all_gather x1, waiting for transfers between devices, shards(): lax.all_gather(w_fc1.astype(jnp.bfloat16), 'shard', axis=0, tiled=True)  86.1 us
    all_gather x1, waiting for transfers between devices, shards(): lax.all_gather(w_fc2.astype(jnp.bfloat16), 'shard', axis=0, tiled=True)  83.5 us
    dot_general x17, matrix products, product(): return jnp.einsum(form, left, right, preferred_element_type=jnp.float32)  71.2 us
    psum x1, blocking collectives, shards(): lax.psum((bias_partial, weight_squares), ('rep', 'shard'))  40 us
    all_gather x1, waiting for transfers between devices, shards(): lax.all_gather(new_pieces[4], 'rep', axis=0, tiled=True)  36.4 us
  transfers between devices with their start and end apart: 33, of which 30 were waited for; matrix products, arithmetic and copies ran while one was open for 11% of the time, Pallas kernels for 0%

profile of v1, /device:TPU:0, one launch (start us, length us, event | category | flops | bytes accessed | tf_op | source)
XLA Modules:
  0.0 1095.6 jit_solution(556863045233779974)
XLA Ops:
  16.6 5.0 collective-permute-start.1
  23.0 4.5 collective-permute-start.3
  28.9 4.7 collective-permute-start.5
  34.9 4.7 collective-permute-start.7
  41.0 4.4 collective-permute-start.9
  46.7 4.4 collective-permute-start.11
  52.5 4.7 collective-permute-start.13
  59.6 4.8 collective-permute-done.14
  65.5 3.5 all-to-all-start
  70.2 5.8 all-to-all-done
  76.8 9.5 all-gather.12.cloned.1.call-done
  86.3 4.7 convolution_bitcast_fusion
  95.0 35.6 %all-gather.14.cloned.1.call-done = bf16[1152,1152]{1,0:T(8,128)(2,1)} async-done(((bf16[72,1152]{1,0:T(8,128)(2,1)}), bf16[1152,1152]{1,0:T(8,128)(2,1)}) %all-gather.14.cloned.1.call-update) | async-done | bytes 2654224 | tf_op jit(solution)/shard_map/all_gather | solution.py:209
  130.6 3.2 fusion.84
  134.6 86.1 %all-gather.16.cloned.1.call-done = bf16[1152,4608]{1,0:T(8,128)(2,1)} async-done(((bf16[72,4608]{1,0:T(8,128)(2,1)}), bf16[1152,4608]{1,0:T(8,128)(2,1)}) %all-gather.16.cloned.1.call-update) | async-done | bytes 10616848 | tf_op jit(solution)/shard_map/all_gather | solution.py:212
  220.7 5.8 convolution_add_fusion
  226.5 83.5 %all-gather.18.cloned.1.call-done = bf16[4608,1152]{1,0:T(8,128)(2,1)} async-done(((bf16[288,1152]{1,0:T(8,128)(2,1)}), bf16[4608,1152]{1,0:T(8,128)(2,1)}) %all-gather.18.cloned.1.call-update) | async-done | bytes 10616848 | tf_op jit(solution)/shard_map/all_gather | solution.py:213
  310.0 8.6 fusion.89
  318.7 4.0 fusion.33
  323.4 7.9 fusion.19
  334.5 3.6 convolution_convert_fusion.4
  348.7 5.6 convolution_convert_fusion.2
  354.4 6.7 convolution_convert_fusion
  362.3 5.9 convolution_convert_fusion.1
  369.2 6.5 fusion.28
  378.9 9.4 all_to_all.29
  390.4 5.4 reduce-scatter.38.cloned.1.call-done
  397.7 100.0 %reduce-scatter.36.cloned.1.call-done = bf16[72,3456]{1,0:T(8,128)(2,1)} async-done(((bf16[1152,3456]{1,0:T(8,128)(2,1)}), bf16[72,3456]{1,0:T(8,128)(2,1)}) %reduce-scatter.36.cloned.1.call-update) | async-done | bytes 497680
  497.8 2.5 copy.107
  500.4 121.7 %reduce-scatter.26.cloned.1.call-done = bf16[288,1152]{1,0:T(8,128)(2,1)} async-done(((bf16[4608,1152]{1,0:T(8,128)(2,1)}), bf16[288,1152]{1,0:T(8,128)(2,1)}) %reduce-scatter.26.cloned.1.call-update) | async-done | bytes 663568 | tf_op jit(solution)/shard_map/reduce_scatter | solution.py:237
  622.1 2.6 copy.111
  624.8 121.7 %reduce-scatter.22.cloned.1.call-done = bf16[72,4608]{1,0:T(8,128)(2,1)} async-done(((bf16[1152,4608]{1,0:T(8,128)(2,1)}), bf16[72,4608]{1,0:T(8,128)(2,1)}) %reduce-scatter.22.cloned.1.call-update) | async-done | bytes 663568 | tf_op jit(solution)/shard_map/reduce_scatter | solution.py:234
  750.2 33.1 %reduce-scatter.34.cloned.1.call-done = f32[576,432]{1,0:T(8,128)} async-done(((f32[1152,432]{1,0:T(8,128)}), f32[576,432]{1,0:T(8,128)}) %reduce-scatter.34.cloned.1.call-update) | async-done | bytes 995344
  785.8 15.5 %reduce-scatter.30.cloned.1.call-done = f32[576,72]{1,0:T(8,128)} async-done(((f32[1152,72]{1,0:T(8,128)}), f32[576,72]{1,0:T(8,128)}) %reduce-scatter.30.cloned.1.call-update) | async-done | bytes 165904
  804.7 27.8 %reduce-scatter.28.cloned.1.call-done = f32[1728,72]{1,0:T(8,128)} async-done(((f32[3456,72]{1,0:T(8,128)}), f32[1728,72]{1,0:T(8,128)}) %reduce-scatter.28.cloned.1.call-update) | async-done | bytes 497680
  837.8 25.2 %reduce-scatter.32.cloned.1.call-done = f32[576,288]{1,0:T(8,128)} async-done(((f32[1152,288]{1,0:T(8,128)}), f32[576,288]{1,0:T(8,128)}) %reduce-scatter.32.cloned.1.call-update) | async-done | bytes 663568
  867.2 22.1 %reduce-scatter.24.cloned.1.call-done = f32[72,2304]{1,0:T(8,128)} async-done(((f32[72,4608]{1,0:T(8,128)}), f32[72,2304]{1,0:T(8,128)}) %reduce-scatter.24.cloned.1.call-update) | async-done | bytes 663568 | tf_op jit(solution)/shard_map/reduce_scatter | solution.py:244
  893.2 40.0 %all-reduce.3 = (f32[]{:T(128)}, f32[16128]{0:T(1024)S(1)}) all-reduce(f32[]{:T(128)S(6)} %add.510, f32[16128]{0:T(1024)S(1)} %constant_dynamic-update-slice_fusion.10), channel_id=1, replica_groups=mesh['rep'=2,'shard'=16] {'rep','shard'}, use_global_device_ids=true, to_apply=%region_32.33 | all-reduce | flops 16129 | bytes 129032 | tf_op jit(solution)/shard_map/psum | solution.py:250
  935.2 3.8 add_bitcast_fusion.1
  939.7 3.3 multiply_add_fusion.3
  945.5 3.9 add_bitcast_fusion
  949.4 30.7 %all-reduce.6.cloned.1.call-done = f32[16,1152]{1,0:T(8,128)} async-done(((f32[16,1152]{1,0:T(8,128)}), f32[16,1152]{1,0:T(8,128)}) %all-reduce.6.cloned.1.call-update) | async-done | bytes 73744
  982.2 2.9 add_bitcast_fusion.2
  985.1 21.1 %all-gather = f32[2,1728,72]{1,2,0:T(8,128)S(1)} all-gather(f32[1,1728,72]{1,2,0:T(8,128)S(1)} %get-tuple-element.56), channel_id=1, replica_groups=mesh['rep'=2,'shard'=16] {'rep'}, dimensions={0}, use_global_device_ids=true | all-gather | bytes 1492992 | tf_op jit(solution)/shard_map/all_gather | solution.py:270
  1009.5 9.2 all-gather.1
  1025.1 19.7 %all-gather.20.cloned.1.call-done = f32[72,4608]{1,0:T(8,128)} async-done(((f32[72,2304]{1,0:T(8,128)}), f32[72,4608]{1,0:T(8,128)}) %all-gather.20.cloned.1.call-update) | async-done | bytes 1327120 | tf_op jit(solution)/shard_map/all_gather | solution.py:272
  1044.7 36.4 %all-gather.24.cloned.1.call-done = f32[2,576,432]{1,2,0:T(8,128)} async-done(((f32[1,576,432]{1,2,0:T(8,128)}), f32[2,576,432]{1,2,0:T(8,128)}) %all-gather.24.cloned.1.call-update) | async-done | bytes 1990672 | tf_op jit(solution)/shard_map/all_gather | solution.py:274
  1081.1 2.8 copy.101
  (302 shorter events, 90.6 us)
Async XLA Ops:
  7.2 79.1 %all-gather.12.cloned.1.call-start = ((), (), s32[]{:S(2)}) async-start(), calls=%async_computation.11 | async-start | bytes 8460288 | tf_op jit(solution)/shard_map/all_gather | solution.py:208
  9.4 121.2 %all-gather.14.cloned.1.call-start = ((), (), s32[]{:S(2)}) async-start(), calls=%async_computation.12 | async-start | bytes 2820096 | tf_op jit(solution)/shard_map/all_gather | solution.py:209
  11.2 209.5 %all-gather.16.cloned.1.call-start = ((), (), s32[]{:S(2)}) async-start(), calls=%async_computation.13 | async-start | bytes 11280384 | tf_op jit(solution)/shard_map/all_gather | solution.py:212
  12.1 52.3 %copy-start.2 = (f32[1152,432]{0,1:T(8,128)S(1)}, f32[1152,432]{0,1:T(8,128)}, u32[]{:S(2)}) copy-start(f32[1152,432]{0,1:T(8,128)} %param.30) | copy-start | bytes 5971972
  12.2 297.8 %all-gather.18.cloned.1.call-start = ((), (), s32[]{:S(2)}) async-start(), calls=%async_computation.14 | async-start | bytes 11280384 | tf_op jit(solution)/shard_map/all_gather | solution.py:213
  16.1 6.7 collective-permute-start
  16.6 6.5 collective-permute-start.1
  22.2 68.8 %copy-start.42 = (f32[128]{0:T(128)}, f32[128]{0:T(128)S(1)}, u32[]{:S(2)}) copy-start(f32[128]{0:T(128)S(1)} %broadcast_multiply_fusion.5) | copy-start | bytes 1540
  22.8 5.8 collective-permute-start.2
  23.0 5.8 collective-permute-start.3
  28.6 6.0 collective-permute-start.4
  28.9 6.1 collective-permute-start.5
  34.6 6.0 collective-permute-start.6
  34.9 6.0 collective-permute-start.7
  40.6 5.7 collective-permute-start.8
  41.0 5.7 collective-permute-start.9
  46.3 5.9 collective-permute-start.10
  46.7 5.8 collective-permute-start.11
  52.3 6.0 collective-permute-start.12
  52.5 7.0 collective-permute-start.13
  58.3 6.1 collective-permute-start.14
  64.4 26.6 %copy-start.21 = (bf16[16,1152]{1,0:T(8,128)(2,1)}, bf16[16,1152]{1,0:T(8,128)(2,1)S(1)}, u32[]{:S(2)}) copy-start(bf16[16,1152]{1,0:T(8,128)(2,1)S(1)} %dynamic_update_slice.63) | copy-start | bytes 110596
  65.5 10.5 all-to-all-start
  69.0 326.8 %reduce-scatter.38.cloned.1.call-start = ((), (), s32[]{:S(2)}) async-start(), calls=%async_computation.27 | async-start | bytes 2820096
  69.6 21.5 %copy-start.50 = (f32[128]{0:T(128)}, f32[128]{0:T(128)S(1)}, u32[]{:S(2)}) copy-start(f32[128]{0:T(128)S(1)} %add_rsqrt_fusion.1) | copy-start | bytes 1540
  76.8 53.8 %copy-start.33 = (f32[1152]{0:T(1024)}, f32[1152]{0:T(1024)S(1)}, u32[]{:S(2)}) copy-start(f32[1152]{0:T(1024)S(1)} %get-tuple-element.38) | copy-start | bytes 13828
  93.3 37.3 %copy-start.66 = (f32[16,128]{1,0:T(8,128)}, f32[16,128]{1,0:T(8,128)S(1)}, u32[]{:S(2)}) copy-start(f32[16,128]{1,0:T(8,128)S(1)} %get-tuple-element.79) | copy-start | bytes 24580
  133.8 86.9 %copy-start.47 = (f32[128]{0:T(128)}, f32[128]{0:T(128)S(1)}, u32[]{:S(2)}) copy-start(f32[128]{0:T(128)S(1)} %broadcast_multiply_fusion.4) | copy-start | bytes 1540
  334.4 163.3 %reduce-scatter.36.cloned.1.call-start = ((), (), s32[]{:S(2)}) async-start(), calls=%async_computation.26 | async-start | bytes 8460288
  354.3 267.8 %reduce-scatter.26.cloned.1.call-start = ((), (), s32[]{:S(2)}) async-start(), calls=%async_computation.17 | async-start | bytes 11280384 | tf_op jit(solution)/shard_map/reduce_scatter | solution.py:237
  361.1 385.5 %reduce-scatter.22.cloned.1.call-start = ((), (), s32[]{:S(2)}) async-start(), calls=%async_computation.15 | async-start | bytes 11280384 | tf_op jit(solution)/shard_map/reduce_scatter | solution.py:234
  368.3 415.0 %reduce-scatter.34.cloned.1.call-start = ((), (), s32[]{:S(2)}) async-start(), calls=%async_computation.24 | async-start | bytes 3538944
  390.3 411.0 %reduce-scatter.30.cloned.1.call-start = ((), (), s32[]{:S(2)}) async-start(), calls=%async_computation.22 | async-start | bytes 884736
  397.7 434.8 %reduce-scatter.28.cloned.1.call-start = ((), (), s32[]{:S(2)}) async-start(), calls=%async_computation.21 | async-start | bytes 2654208
  500.3 362.6 %reduce-scatter.32.cloned.1.call-start = ((), (), s32[]{:S(2)}) async-start(), calls=%async_computation.23 | async-start | bytes 2654208
  624.7 124.3 %copy-start.38 = (f32[16,72]{1,0:T(8,128)S(1)}, f32[16,72]{1,0:T(8,128)}, u32[]{:S(2)}) copy-start(f32[16,72]{1,0:T(8,128)} %get-tuple-element.73) | copy-start | bytes 13828
  624.7 124.3 %copy-start.57 = (f32[16,72]{1,0:T(8,128)S(1)}, f32[16,72]{1,0:T(8,128)}, u32[]{:S(2)}) copy-start(f32[16,72]{1,0:T(8,128)} %get-tuple-element.71) | copy-start | bytes 13828
  624.7 124.5 %copy-start.56 = (f32[1152]{0:T(1024)S(1)}, f32[1152]{0:T(1024)}, u32[]{:S(2)}) copy-start(f32[1152]{0:T(1024)} %get-tuple-element.69) | copy-start | bytes 13828
  624.7 124.5 %copy-start.41 = (f32[4608]{0:T(1024)S(1)}, f32[4608]{0:T(1024)}, u32[]{:S(2)}) copy-start(f32[4608]{0:T(1024)} %get-tuple-element.86) | copy-start | bytes 55300
  624.7 124.5 %copy-start.55 = (f32[1152]{0:T(1024)S(1)}, f32[1152]{0:T(1024)}, u32[]{:S(2)}) copy-start(f32[1152]{0:T(1024)} %get-tuple-element.31) | copy-start | bytes 13828
  624.8 124.5 %copy-start.3 = (f32[1152,432]{0,1:T(8,128)S(1)}, f32[1152,432]{0,1:T(8,128)}, u32[]{:S(2)}) copy-start(f32[1152,432]{0,1:T(8,128)} %param.30) | copy-start | bytes 5971972
  624.8 264.5 %reduce-scatter.24.cloned.1.call-start = ((), (), s32[]{:S(2)}) async-start(), calls=%async_computation.16 | async-start | bytes 1990656 | tf_op jit(solution)/shard_map/reduce_scatter | solution.py:244
  748.8 231.3 %all-reduce.6.cloned.1.call-start = ((), (), s32[]{:S(2)}) async-start(), calls=%async_computation.25 | async-start | bytes 147456
  893.1 127.4 %all-gather.22.cloned.1.call-start = ((), (), s32[]{:S(2)}) async-start(), calls=%async_computation.19 | async-start | bytes 2211840 | tf_op jit(solution)/shard_map/all_gather | solution.py:273
  939.0 105.7 %all-gather.20.cloned.1.call-start = ((), (), s32[]{:S(2)}) async-start(), calls=%async_computation.18 | async-start | bytes 1990656 | tf_op jit(solution)/shard_map/all_gather | solution.py:272
  943.0 138.1 %all-gather.24.cloned.1.call-start = ((), (), s32[]{:S(2)}) async-start(), calls=%async_computation.20 | async-start | bytes 3317760 | tf_op jit(solution)/shard_map/all_gather | solution.py:274
  945.5 34.7 %copy-start.45 = (f32[1,1152]{1,0:T(1,128)S(1)}, f32[1,1152]{1,0:T(1,128)}, u32[]{:S(2)}) copy-start(f32[1,1152]{1,0:T(1,128)} %get-tuple-element.63) | copy-start | bytes 13828
  945.5 34.7 %copy-start.46 = (f32[1,1152]{1,0:T(1,128)S(1)}, f32[1,1152]{1,0:T(1,128)}, u32[]{:S(2)}) copy-start(f32[1,1152]{1,0:T(1,128)} %get-tuple-element.64) | copy-start | bytes 13828
  (53 other events, 262.9 us)
Sparse Core Ops, SparseCore 0:
  10.8 75.5 all-gather.11
  89.1 41.4 all-gather.13
  133.5 87.1 all-gather.15
  223.4 86.5 all-gather.17
  334.6 61.1 reduce-scatter.37
  399.7 98.0 reduce-scatter.35
  501.8 120.2 reduce-scatter.25
  626.2 120.3 reduce-scatter.21
  748.8 34.3 reduce-scatter.33
  785.9 15.3 reduce-scatter.29
  804.2 28.2 reduce-scatter.27
  834.6 28.3 reduce-scatter.31
  865.8 23.4 reduce-scatter.23
  893.3 86.8 all-reduce.5
  982.1 35.6 all-gather.21
  1019.8 24.8 all-gather.19
  1046.7 34.3 all-gather.23
